TPU v7x, 32 devices: a whole 2x2x4 slice. The times are simulated.
32 devices in a mesh: scene: 2 (over y), tok: 4 (over z), col: 2 (over x), rep: 2 (over core).
Axes of the slice: x: 2, y: 2, z: 4, core: 2. Of those that a mesh axis runs over, the one named last changes fastest.
Arguments:
- tokens: float32 [8192, 512], P(('scene', 'tok'), ('col', 'rep')), parts along dimension 0
- w_qkv: float32 [2, 3, 512, 512], P(None, None, None, ('col', 'rep'))
- w_out: float32 [2, 512, 512], P(None, ('col', 'rep')), may hold values from -0.25 to 0.25
- w_up: float32 [2, 512, 2048], P(None, None, ('col', 'rep')), may hold values from -0.25 to 0.25
- w_down: float32 [2, 2048, 512], P(None, ('col', 'rep')), may hold values from -0.125 to 0.125
- attn_gain: float32 [2, 512], replicated, may hold values from 0.1 to 1.9
- mlp_gain: float32 [2, 512], replicated, may hold values from 0.1 to 1.9
- dest_device: int32 [128], P(('scene', 'tok')), parts along dimension 0, may hold values from 0 to 3, as said below
- dest_slot: int32 [128], P(('scene', 'tok')), parts along dimension 0, may hold values from 0 to 15, as said below
- pillar: int32 [8192], P(('scene', 'tok')), parts along dimension 0, may hold values from -1 to 2047, as said below
- depth_weight: float32 [2, 3, 3, 512], replicated, may hold values from -2 to 2
- point_weight: float32 [2, 512, 1024], replicated, may hold values from -0.25 to 0.25
- raster_gain: float32 [2, 512], replicated, may hold values from 0.1 to 1.9
Outputs:
- raster: float32 [128, 32, 512], P(('scene', 'tok', 'rep'), 'col'), parts along dimension 0
There are 2 independent parts, one for each index of `scene`. A program takes and returns all parts, laid end to end along the dimension named above; an argument that names none is the same for every part. Nothing has to cross between parts.
Inputs may be any that keep to these rules, and one draw needn't show every extreme that they name: `dest_device`: together with dest_slot the blocks fill every index of tok's 16 slots exactly once. At most 5 blocks of one index of tok go to one index, and every index sends exactly 5 blocks to some index. `dest_slot`: the slot of the block among the 16 of its destination. The token at Hilbert position t has a cell in raster rows i * 16 to (i + 1) * 16 - 1 with i = t // 1024, or -1 if it has no pillar; several tokens may share a cell.
All inputs are finite; a program needn't handle non-finite values.
Results may differ from a plain program's by a relative error of at most 0.00012.
Values sent between devices are 32-bit elements; how exact they have to be, the bound alone decides.
A program may use at most 128 MiB of HBM per device.

v0:
```python
import jax
import jax.numpy as jnp
from jax import lax
from jax.sharding import PartitionSpec as P

PATCH = 1024
TR = 16
TC = 16
HD = 16
MATMUL_PRECISION = lax.Precision.HIGHEST
EPSILON = 1e-05


def padded(block, sides, width):
    for axis, dim in sides:
        count = lax.axis_size(axis)
        forward = [(i, i + 1) for i in range(count - 1)]
        backward = [(target, source) for source, target in forward]
        low = lax.ppermute(
            lax.slice_in_dim(block, block.shape[dim] - width, None, axis=dim), axis, forward
        )
        high = lax.ppermute(lax.slice_in_dim(block, 0, width, axis=dim), axis, backward)
        block = jnp.concatenate([low, block, high], axis=dim)
    return block


def layer_norm(values, gain_row):
    average = jnp.mean(values, axis=-1, keepdims=True)
    centered = values - average
    variance = jnp.mean(centered * centered, axis=-1, keepdims=True)
    return centered * lax.rsqrt(variance + EPSILON) * gain_row


def patch_attention(query_projection, key_proj, value_proj):
    scores = jnp.einsum(
        "qhd,khd->hqk", query_projection, key_proj, precision=MATMUL_PRECISION
    ) * HD ** (-0.5)
    scores = scores - jnp.max(scores, axis=-1, keepdims=True)
    weights = jnp.exp(scores)
    weights = weights / jnp.sum(weights, axis=-1, keepdims=True)
    return jnp.einsum("hqk,khd->qhd", weights, value_proj, precision=MATMUL_PRECISION)


def matmul(left, right):
    return jnp.dot(left, right, precision=MATMUL_PRECISION, preferred_element_type=jnp.float32)


def widen(slice_cols):
    return lax.all_gather(slice_cols, ("col", "rep"), axis=1, tiled=True)


def block_layer(stream, layer_index, w_qkv, w_out, w_up, w_down, attn_gain, mlp_gain):
    row_count = stream.shape[0]
    local_cols = w_qkv.shape[-1]
    heads_here = local_cols // HD
    normed = layer_norm(stream, attn_gain[layer_index])
    shaped = tuple(
        (
            matmul(normed, w_qkv[layer_index, j]).reshape(row_count // PATCH, PATCH, heads_here, HD)
            for j in range(3)
        )
    )

    def attend_patch(operands):
        return patch_attention(operands[0], operands[1], operands[2]).reshape(PATCH, local_cols)

    attended = lax.map(attend_patch, shaped).reshape(row_count, local_cols)
    partial_out = matmul(attended, w_out[layer_index])
    stream = stream + lax.psum(partial_out, ("col", "rep"))
    normed = layer_norm(stream, mlp_gain[layer_index])
    hidden = jax.nn.gelu(matmul(normed, w_up[layer_index]), approximate=False)
    partial_mlp = matmul(hidden, w_down[layer_index])
    summed_share = lax.psum_scatter(partial_mlp, ("col", "rep"), scatter_dimension=1, tiled=True)
    feature_width = summed_share.shape[1]
    own_cols = lax.dynamic_slice_in_dim(
        stream, lax.axis_index(("col", "rep")) * feature_width, feature_width, 1
    )
    return own_cols + summed_share


def send_blocks(block_list, dest_device, dest_slot):
    block_count, rows_per_block, feature_width = block_list.shape
    peers = lax.axis_size("tok")
    capacity = max(2, (block_count + peers - 4) // (peers - 1))
    order_index = jnp.arange(block_count, dtype=jnp.int32)
    earlier = (dest_device[:, None] == dest_device[None, :]) & (
        order_index[None, :] < order_index[:, None]
    )
    prior_count = jnp.sum(earlier.astype(jnp.int32), axis=1)
    slot_key = dest_device * capacity + prior_count
    select_entries = (
        jnp.arange(peers * capacity, dtype=jnp.int32)[:, None] == slot_key[None, :]
    ).astype(jnp.float32)
    outgoing = jnp.einsum(
        "jb,brf->jrf", select_entries, block_list, precision=MATMUL_PRECISION
    ).reshape(peers, capacity, rows_per_block, feature_width)
    slot_codes = matmul(select_entries, (dest_slot + 1).astype(jnp.float32)).reshape(
        peers, capacity
    )
    incoming, arrived = (
        lax.all_to_all(outgoing, "tok", split_axis=0, concat_axis=0, tiled=True),
        lax.all_to_all(slot_codes, "tok", split_axis=0, concat_axis=0, tiled=True),
    )
    wanted = (order_index + 1).astype(jnp.float32)
    placing = (wanted[:, None] == arrived.reshape(-1)[None, :]).astype(jnp.float32)
    flat_incoming = incoming.reshape(peers * capacity, rows_per_block, feature_width)
    return jnp.einsum("sj,jrf->srf", placing, flat_incoming, precision=MATMUL_PRECISION)


def raster_cells(extended, depth_weight, point_weight, gain_row):
    row_count = extended.shape[0] - 2
    col_count = extended.shape[1] - 2
    count_of_channels = extended.shape[2]
    normed = (
        extended
        * lax.rsqrt(jnp.mean(extended * extended, axis=-1, keepdims=True) + EPSILON)
        * gain_row
    )
    mixed_cells = jnp.zeros((row_count, col_count, count_of_channels), jnp.float32)
    for row_tap in range(3):
        for col_tap in range(3):
            mixed_cells = (
                mixed_cells
                + normed[row_tap : row_tap + row_count, col_tap : col_tap + col_count]
                * depth_weight[row_tap, col_tap]
            )
    combined = matmul(mixed_cells.reshape(row_count * col_count, count_of_channels), point_weight)
    combined = combined.reshape(row_count, col_count, 2 * count_of_channels)
    centre = extended[1:-1, 1:-1]
    return centre + combined[..., :count_of_channels] * jax.nn.sigmoid(
        combined[..., count_of_channels:]
    )


def on_device(
    tokens,
    w_qkv,
    w_out,
    w_up,
    w_down,
    attn_gain,
    mlp_gain,
    dest_device,
    dest_slot,
    pillar,
    depth_weight,
    point_weight,
    raster_gain,
):
    stream = widen(tokens)
    first_out = block_layer(stream, 0, w_qkv, w_out, w_up, w_down, attn_gain, mlp_gain)
    feature_width = first_out.shape[1]
    block_count = dest_device.shape[0]
    block_list = first_out.reshape(block_count, first_out.shape[0] // block_count, feature_width)
    reordered_tokens = send_blocks(block_list, dest_device, dest_slot)
    stream = widen(reordered_tokens.reshape(-1, feature_width))
    stream = widen(block_layer(stream, 1, w_qkv, w_out, w_up, w_down, attn_gain, mlp_gain))
    rep_rows = TR // lax.axis_size("rep")
    row_start = lax.axis_index(("tok", "rep")) * rep_rows
    col_start = lax.axis_index("col") * TC
    full_width = TC * lax.axis_size("col")
    cell_rows = row_start + jnp.arange(rep_rows, dtype=jnp.int32)[:, None]
    cell_ids = (
        cell_rows * full_width + col_start + jnp.arange(TC, dtype=jnp.int32)[None, :]
    ).reshape(-1)
    onehot = (pillar[:, None] == cell_ids[None, :]).astype(jnp.float32)
    raster = jnp.einsum("tc,td->cd", onehot, stream, precision=MATMUL_PRECISION).reshape(
        rep_rows, TC, -1
    )
    for layer_index in range(2):
        extended = padded(raster, ((("tok", "rep"), 0), ("col", 1)), 1)
        raster = raster_cells(
            extended, depth_weight[layer_index], point_weight[layer_index], raster_gain[layer_index]
        )
    return raster


def solution(mesh):
    placed = (
        P(("scene", "tok"), ("col", "rep")),
        P(None, None, None, ("col", "rep")),
        P(None, ("col", "rep"), None),
        P(None, None, ("col", "rep")),
        P(None, ("col", "rep"), None),
        P(),
        P(),
        P(("scene", "tok")),
        P(("scene", "tok")),
        P(("scene", "tok")),
        P(),
        P(),
        P(),
    )
    return jax.shard_map(
        on_device,
        mesh=mesh,
        in_specs=placed,
        out_specs=P(("scene", "tok", "rep"), "col", None),
        check_vma=False,
    )
```

profile of v0, /device:TPU:1, one launch (start us, length us, event | category | flops | bytes accessed | tf_op | source)
XLA Modules:
  0.0 510.4 jit_solution(3229951573968464027)
XLA Ops:
  9.9 24.3 %all-gather.4.cloned.1.call-done = f32[1024,512]{1,0:T(8,128)} async-done(((f32[1024,128]{1,0:T(8,128)}), f32[1024,512]{1,0:T(8,128)}) %all-gather.4.cloned.1.call-update) | async-done | bytes 2097168 | tf_op jit(solution)/shard_map/all_gather | solution.py:49
  42.0 28.0 %multiply_reduce_fusion.1 = (f32[8,1024]{1,0:T(8,128)S(1)}, f32[8,1024,1024]{1,2,0:T(8,128)S(1)}) fusion(f32[1024,8,16]{0,2,1:T(8,128)S(1)} %fusion.32, f32[1024,8,16]{0,2,1:T(8,128)S(1)} %fusion.30), kind=kOutput, calls=%fused_computation.7 | convolution fusion | flops 1627381760 | bytes 34635776 | tf_op jit(solution)/shard_map/while/body/eval_jaxpr/qhd,khd->hqk/dot_general | solution.py:35
  70.0 5.9 %fusion.4 = f32[8,1024]{1,0:T(8,128)S(1)} fusion(f32[8,1024,1024]{1,2,0:T(8,128)S(1)} %get-tuple-element.80, f32[8,1024]{1,0:T(8,128)S(1)} %get-tuple-element.79), kind=kLoop, calls=%fused_computation.8 | loop fusion | flops 25157632 | bytes 33619968 | tf_op jit(solution)/shard_map/while/body/eval_jaxpr/reduce_sum | solution.py:40
  75.9 5.2 %copy-done = f32[8,1024,1024]{1,2,0:T(8,128)} copy-done((f32[8,1024,1024]{1,2,0:T(8,128)}, f32[8,1024,1024]{1,2,0:T(8,128)S(1)}, u32[]{:S(2)}) %copy-start) | copy-done | bytes 33554456
  84.4 25.6 %fusion.2 = f32[8,16,1024]{2,1,0:T(8,128)S(1)} fusion(f32[1024,8,16]{0,2,1:T(8,128)} %fusion.34, f32[8,1024,1024]{1,2,0:T(8,128)} %copy-done, f32[8,1024]{1,0:T(8,128)S(1)} %fusion.4, f32[8,1024]{1,0:T(8,128)S(1)} %get-tuple-element.79), kind=kOutput, calls=%fused_computation.4 | convolution fusion | flops 1635778560 | bytes 34668544 | tf_op jit(solution)/shard_map/while/body/eval_jaxpr/hqk,khd->qhd/dot_general | solution.py:41
  110.0 4.1 fusion.299
  114.3 50.8 %all-reduce.3.cloned.1.call-done = f32[1024,512]{1,0:T(8,128)} async-done(((f32[1024,512]{1,0:T(8,128)}), f32[1024,512]{1,0:T(8,128)}) %all-reduce.3.cloned.1.call-update) | async-done | bytes 2097168 | tf_op jit(solution)/shard_map/psum | solution.py:69
  169.3 3.7 fusion.143
  173.0 9.5 %fusion.14 = f32[1024,512]{1,0:T(8,128)} fusion(f32[1024,512]{1,0:T(8,128)S(1)} %fusion.143, f32[2,512,512]{2,1,0:T(8,128)S(1)} %copy-done.15), kind=kOutput, calls=%fused_computation.20 | convolution fusion | flops 3254779904 | bytes 5242880 | tf_op jit(solution)/shard_map/dot_general | solution.py:45
  184.1 4.3 all-to-all-start
  188.5 25.5 %reduce-scatter.3.cloned.1.call-done = f32[1024,128]{1,0:T(8,128)} async-done(((f32[1024,512]{1,0:T(8,128)}), f32[1024,128]{1,0:T(8,128)}) %reduce-scatter.3.cloned.1.call-update) | async-done | bytes 524304 | tf_op jit(solution)/shard_map/reduce_scatter | solution.py:73
  217.1 4.3 all-to-all-start.1
  222.7 15.6 %all-to-all-done.1 = f32[4,5,64,128]{3,2,1,0:T(8,128)S(1)} async-done(((f32[4,5,64,128]{3,2,1,0:T(8,128)}), f32[4,5,64,128]{3,2,1,0:T(8,128)S(1)}, u32[]{:S(2)}, u32[]{:S(2)}) %all-to-all-start.1) | async-done | bytes 655392 | tf_op jit(solution)/shard_map/all_to_all | solution.py:101
  240.6 21.8 %all-gather.6.cloned.1.call-done = f32[1024,512]{1,0:T(8,128)} async-done(((f32[1024,128]{1,0:T(8,128)}), f32[1024,512]{1,0:T(8,128)}) %all-gather.6.cloned.1.call-update) | async-done | bytes 2097168 | tf_op jit(solution)/shard_map/all_gather | solution.py:49
  270.1 27.9 %multiply_reduce_fusion = (f32[8,1024]{1,0:T(8,128)S(1)}, f32[8,1024,1024]{1,2,0:T(8,128)S(1)}) fusion(f32[1024,8,16]{0,2,1:T(8,128)S(1)} %fusion.26, f32[1024,8,16]{0,2,1:T(8,128)S(1)} %fusion.24), kind=kOutput, calls=%fused_computation.6 | convolution fusion | flops 1627381760 | bytes 34635776 | tf_op jit(solution)/shard_map/while/body/eval_jaxpr/qhd,khd->hqk/dot_general | solution.py:35
  298.0 5.9 %fusion.5 = f32[8,1024]{1,0:T(8,128)S(1)} fusion(f32[8,1024,1024]{1,2,0:T(8,128)S(1)} %get-tuple-element.82, f32[8,1024]{1,0:T(8,128)S(1)} %get-tuple-element.81), kind=kLoop, calls=%fused_computation.9 | loop fusion | flops 25157632 | bytes 33619968 | tf_op jit(solution)/shard_map/while/body/eval_jaxpr/reduce_sum | solution.py:40
  303.9 5.2 %copy-done.1 = f32[8,1024,1024]{1,2,0:T(8,128)} copy-done((f32[8,1024,1024]{1,2,0:T(8,128)}, f32[8,1024,1024]{1,2,0:T(8,128)S(1)}, u32[]{:S(2)}) %copy-start.1) | copy-done | bytes 33554456
  311.7 25.0 %fusion = f32[8,16,1024]{2,1,0:T(8,128)S(1)} fusion(f32[1024,8,16]{0,2,1:T(8,128)S(1)} %fusion.28, f32[8,1024,1024]{1,2,0:T(8,128)} %copy-done.1, f32[8,1024]{1,0:T(8,128)S(1)} %fusion.5, f32[8,1024]{1,0:T(8,128)S(1)} %get-tuple-element.81), kind=kOutput, calls=%fused_computation.2 | convolution fusion | flops 1635778560 | bytes 34668544 | tf_op jit(solution)/shard_map/while/body/eval_jaxpr/hqk,khd->qhd/dot_general | solution.py:41
  336.7 4.1 fusion.297
  340.8 50.8 %all-reduce.5.cloned.1.call-done = f32[1024,512]{1,0:T(8,128)} async-done(((f32[1024,512]{1,0:T(8,128)}), f32[1024,512]{1,0:T(8,128)}) %all-reduce.5.cloned.1.call-update) | async-done | bytes 2097168 | tf_op jit(solution)/shard_map/psum | solution.py:69
  395.9 3.7 fusion.89
  399.6 9.5 %fusion.18 = f32[1024,512]{1,0:T(8,128)} fusion(f32[1024,512]{1,0:T(8,128)S(1)} %fusion.89, f32[2,512,512]{2,1,0:T(8,128)S(1)} %copy-done.16), kind=kOutput, calls=%fused_computation.23 | convolution fusion | flops 3254779904 | bytes 5242880 | tf_op jit(solution)/shard_map/dot_general | solution.py:45
  409.2 31.4 %reduce-scatter.5.cloned.1.call-done = f32[1024,128]{1,0:T(8,128)} async-done(((f32[1024,512]{1,0:T(8,128)}), f32[1024,128]{1,0:T(8,128)}) %reduce-scatter.5.cloned.1.call-update) | async-done | bytes 524304 | tf_op jit(solution)/shard_map/reduce_scatter | solution.py:73
  442.9 23.3 %all-gather.8.cloned.1.call-done = f32[1024,512]{1,0:T(8,128)} async-done(((f32[1024,128]{1,0:T(8,128)}), f32[1024,512]{1,0:T(8,128)}) %all-gather.8.cloned.1.call-update) | async-done | bytes 2097168 | tf_op jit(solution)/shard_map/all_gather | solution.py:49
  (136 shorter events, 80.7 us)
Async XLA Ops:
  6.5 27.7 %all-gather.4.cloned.1.call-start = ((), (), s32[]{:S(2)}) async-start(), calls=%async_computation.4 | async-start | bytes 2621440 | tf_op jit(solution)/shard_map/all_gather | solution.py:49
  7.3 157.8 %all-reduce.3.cloned.1.call-start = ((), (), s32[]{:S(2)}) async-start(), calls=%async_computation.5 | async-start | bytes 4194304 | tf_op jit(solution)/shard_map/psum | solution.py:69
  70.0 11.1 %copy-start = (f32[8,1024,1024]{1,2,0:T(8,128)}, f32[8,1024,1024]{1,2,0:T(8,128)S(1)}, u32[]{:S(2)}) copy-start(f32[8,1024,1024]{1,2,0:T(8,128)S(1)} %get-tuple-element.80) | copy-start | bytes 100663296
  114.2 99.8 %reduce-scatter.3.cloned.1.call-start = ((), (), s32[]{:S(2)}) async-start(), calls=%async_computation.6 | async-start | bytes 2621440 | tf_op jit(solution)/shard_map/reduce_scatter | solution.py:73
  184.1 33.0 %all-to-all-start = ((f32[4,1,5]{2,1,0:T(1,128)}), f32[4,1,5]{2,1,0:T(1,128)S(1)}, u32[]{:S(2)}, u32[]{:S(2)}) async-start(f32[4,1,5]{2,1,0:T(1,128)} %bitcast.2), calls=%async_computation | async-start | bytes 4096 | tf_op jit(solution)/shard_map/all_to_all | solution.py:102
  217.1 21.2 %all-to-all-start.1 = ((f32[4,5,64,128]{3,2,1,0:T(8,128)}), f32[4,5,64,128]{3,2,1,0:T(8,128)S(1)}, u32[]{:S(2)}, u32[]{:S(2)}) async-start(f32[4,5,64,128]{3,2,1,0:T(8,128)} %copy.48), calls=%async_computation.2 | async-start | bytes 1310720 | tf_op jit(solution)/shard_map/all_to_all | solution.py:101
  221.5 40.9 %all-gather.6.cloned.1.call-start = ((), (), s32[]{:S(2)}) async-start(), calls=%async_computation.7 | async-start | bytes 2621440 | tf_op jit(solution)/shard_map/all_gather | solution.py:49
  240.1 151.6 %all-reduce.5.cloned.1.call-start = ((), (), s32[]{:S(2)}) async-start(), calls=%async_computation.8 | async-start | bytes 4194304 | tf_op jit(solution)/shard_map/psum | solution.py:69
  298.0 11.1 %copy-start.1 = (f32[8,1024,1024]{1,2,0:T(8,128)}, f32[8,1024,1024]{1,2,0:T(8,128)S(1)}, u32[]{:S(2)}) copy-start(f32[8,1024,1024]{1,2,0:T(8,128)S(1)} %get-tuple-element.82) | copy-start | bytes 100663296
  340.8 99.8 %reduce-scatter.5.cloned.1.call-start = ((), (), s32[]{:S(2)}) async-start(), calls=%async_computation.9 | async-start | bytes 2621440 | tf_op jit(solution)/shard_map/reduce_scatter | solution.py:73
  393.6 6.0 %copy-start.5 = (f32[1024,512]{1,0:T(8,128)}, f32[1024,512]{1,0:T(8,128)S(1)}, u32[]{:S(2)}) copy-start(f32[1024,512]{1,0:T(8,128)S(1)} %get-tuple-element.24) | copy-start | bytes 6291460
  409.1 33.7 %copy-start.9 = (f32[2,3,3,512]{3,0,2,1:T(2,128)S(1)}, f32[2,3,3,512]{3,0,2,1:T(2,128)}, u32[]{:S(2)}) copy-start(f32[2,3,3,512]{3,0,2,1:T(2,128)} %param.23) | copy-start | bytes 110596
  409.1 57.1 %copy-start.13 = (s32[1024]{0:T(1024)S(1)}, s32[1024]{0:T(1024)}, u32[]{:S(2)}) copy-start(s32[1024]{0:T(1024)} %param.22) | copy-start | bytes 12292
  409.1 57.1 %all-gather.8.cloned.1.call-start = ((), (), s32[]{:S(2)}) async-start(), calls=%async_computation.10 | async-start | bytes 2621440 | tf_op jit(solution)/shard_map/all_gather | solution.py:49
  442.7 38.5 %copy-start.12 = (f32[2,512]{1,0:T(2,128)S(1)}, f32[2,512]{1,0:T(2,128)}, u32[]{:S(2)}) copy-start(f32[2,512]{1,0:T(2,128)} %param.25) | copy-start | bytes 12292
  466.3 18.4 %copy-start.14 = (f32[2,512,1024]{2,1,0:T(8,128)S(1)}, f32[2,512,1024]{2,1,0:T(8,128)}, u32[]{:S(2)}) copy-start(f32[2,512,1024]{2,1,0:T(8,128)} %param.24) | copy-start | bytes 12582916
  469.1 5.2 %collective-permute-start = (f32[1,16,512]{2,1,0:T(8,128)S(1)}, f32[1,16,512]{2,1,0:T(8,128)S(1)}, u32[]{:S(2)}, u32[]{:S(2)}) collective-permute-start(f32[1,16,512]{2,1,0:T(8,128)S(1)} %get-tuple-element.51), channel_id=1, source_target_pairs={{0,1},{1,4},{4,5},{5,8},{8,9},{9,12},{12,13},{2,3},{3,6},{6,7},{7,... | collective-permute-start | bytes 98312 | tf_op jit(solution)/shard_map/ppermute | solution.py:19
  472.4 5.2 %collective-permute-start.1 = (f32[1,16,512]{2,1,0:T(8,128)S(1)}, f32[1,16,512]{2,1,0:T(8,128)S(1)}, u32[]{:S(2)}, u32[]{:S(2)}) collective-permute-start(f32[1,16,512]{2,1,0:T(8,128)S(1)} %get-tuple-element.52), channel_id=1, source_target_pairs={{1,0},{4,1},{5,4},{8,5},{9,8},{12,9},{13,12},{3,2},{6,3},{7,6},{10... | collective-permute-start | bytes 98312 | tf_op jit(solution)/shard_map/ppermute | solution.py:22
  477.6 3.5 collective-permute-start.2
  479.8 4.5 collective-permute-start.3
  486.2 5.3 %collective-permute-start.4 = (f32[1,16,512]{2,1,0:T(8,128)S(1)}, f32[1,16,512]{2,1,0:T(8,128)S(1)}, u32[]{:S(2)}, u32[]{:S(2)}) collective-permute-start(f32[1,16,512]{2,1,0:T(8,128)S(1)} %get-tuple-element.49), channel_id=1, source_target_pairs={{0,1},{1,4},{4,5},{5,8},{8,9},{9,12},{12,13},{2,3},{3,6},{6,7},{7,... | collective-permute-start | bytes 98312 | tf_op jit(solution)/shard_map/ppermute | solution.py:19
  489.6 5.2 %collective-permute-start.5 = (f32[1,16,512]{2,1,0:T(8,128)S(1)}, f32[1,16,512]{2,1,0:T(8,128)S(1)}, u32[]{:S(2)}, u32[]{:S(2)}) collective-permute-start(f32[1,16,512]{2,1,0:T(8,128)S(1)} %get-tuple-element.50), channel_id=1, source_target_pairs={{1,0},{4,1},{5,4},{8,5},{9,8},{12,9},{13,12},{3,2},{6,3},{7,6},{10... | collective-permute-start | bytes 98312 | tf_op jit(solution)/shard_map/ppermute | solution.py:22
  494.9 2.7 collective-permute-start.6
  496.2 4.5 collective-permute-start.7
  (12 other events, 33.8 us)
Sparse Core Ops, SparseCore 0:
  8.9 25.2 all-gather.3
  114.3 50.7 all-reduce.2
  182.6 31.3 reduce-scatter.2
  240.2 22.0 all-gather.5
  340.9 50.7 all-reduce.4
  409.3 31.2 reduce-scatter.4
  442.8 23.4 all-gather.7
where the time goes:
time: 515 us; the launch traced here: 510 us
  waiting for transfers between devices  257 us (50%)
  matrix products  165 us (32%)
  other arithmetic  27 us (5%)
  starting transfers between devices  25.4 us (5%)
  local copies, waits for them, and re-layouts  21.6 us (4%)
  between operations  14.3 us (3%)
    psum x2, waiting for transfers between devices, block_layer(): stream = stream + lax.psum(partial_out, ('col', 'rep'))  102 us
    all_gather x3, waiting for transfers between devices, widen(): return lax.all_gather(slice_cols, ('col', 'rep'), axis=1, tiled=True)  69.4 us
    reduce_scatter x2, waiting for transfers between devices, block_layer(): lax.psum_scatter(partial_mlp, ('col', 'rep'), scatter_dimension=1, tiled=...  56.9 us
    dot_general x2, matrix products, patch_attention(): jnp.einsum('qhd,khd->hqk', query_projection, key_proj, precision=MATMUL_P...  56 us
    dot_general x15, matrix products, matmul(): jnp.dot(left, right, precision=MATMUL_PRECISION, preferred_element_type=j...  53.7 us
    dot_general x2, matrix products, patch_attention(): jnp.einsum('hqk,khd->qhd', weights, value_proj, precision=MATMUL_PRECISION)  50.6 us
    unnamed x45, local copies, waits for them, and re-layouts  16.8 us
    all_to_all x1, waiting for transfers between devices, send_blocks(): lax.all_to_all(outgoing, 'tok', split_axis=0, concat_axis=0, tiled=True)  15.6 us
  transfers between devices with their start and end apart: 17, of which 12 were waited for; matrix products, arithmetic and copies ran while one was open for 2% of the time, Pallas kernels for 0%

commit v1 on v0

--- a/solution.py
+++ b/solution.py
@@ -1,7 +1,9 @@
+import functools
 import jax
 import jax.numpy as jnp
 from jax import lax
 from jax.sharding import PartitionSpec as P
+from jax.lax import psum
 
 PATCH = 1024
 TR = 16
@@ -9,6 +11,15 @@
 HD = 16
 MATMUL_PRECISION = lax.Precision.HIGHEST
 EPSILON = 1e-05
+
+
+def begin_quotas(vals, named_axis, shard_axis):
+    for q in (named_axis, shard_axis):
+        vals = psum(vals, axis_name=q)
+    return vals
+
+
+gates_part = functools.partial(begin_quotas, named_axis="rep", shard_axis="col")
 
 
 def padded(block, sides, width):
@@ -66,7 +77,7 @@
 
     attended = lax.map(attend_patch, shaped).reshape(row_count, local_cols)
     partial_out = matmul(attended, w_out[layer_index])
-    stream = stream + lax.psum(partial_out, ("col", "rep"))
+    stream = stream + gates_part(partial_out)
     normed = layer_norm(stream, mlp_gain[layer_index])
     hidden = jax.nn.gelu(matmul(normed, w_up[layer_index]), approximate=False)
     partial_mlp = matmul(hidden, w_down[layer_index])

time: 515 us -> 588 us (1.14)
  waiting for transfers between devices: 257 us -> 330 us
    psum x2 -> x4, waiting for transfers between devices: 102 us -> 174 us  [begin_quotas(): vals = psum(vals, axis_name=q)]
  transfers between devices with their start and end apart: 17 -> 19, of which waited for: 12 -> 14; matrix products, arithmetic and copies ran while one was open for 2% -> 1% of each run, Pallas kernels for 0% -> 0%
where the time goes in v1:
time: 588 us; the launch traced here: 583 us
  waiting for transfers between devices  330 us (56%)
  matrix products  165 us (28%)
  other arithmetic  27 us (5%)
  starting transfers between devices  25.5 us (4%)
  local copies, waits for them, and re-layouts  21.6 us (4%)
  between operations  14 us (2%)
    psum x4, waiting for transfers between devices, begin_quotas(): vals = psum(vals, axis_name=q)  174 us
    all_gather x3, waiting for transfers between devices, widen(): return lax.all_gather(slice_cols, ('col', 'rep'), axis=1, tiled=True)  69.4 us
    reduce_scatter x2, waiting for transfers between devices, block_layer(): lax.psum_scatter(partial_mlp, ('col', 'rep'), scatter_dimension=1, tiled=...  56.7 us
    dot_general x2, matrix products, patch_attention(): jnp.einsum('qhd,khd->hqk', query_projection, key_proj, precision=MATMUL_P...  56 us
    dot_general x15, matrix products, matmul(): jnp.dot(left, right, precision=MATMUL_PRECISION, preferred_element_type=j...  53.7 us
    dot_general x2, matrix products, patch_attention(): jnp.einsum('hqk,khd->qhd', weights, value_proj, precision=MATMUL_PRECISION)  50.6 us
    unnamed x45, local copies, waits for them, and re-layouts  16.8 us
    all_to_all x1, waiting for transfers between devices, send_blocks(): lax.all_to_all(outgoing, 'tok', split_axis=0, concat_axis=0, tiled=True)  15.6 us
  transfers between devices with their start and end apart: 19, of which 14 were waited for; matrix products, arithmetic and copies ran while one was open for 1% of the time, Pallas kernels for 0%

profile of v1, /device:TPU:1, one launch (start us, length us, event | category | flops | bytes accessed | tf_op | source)
XLA Modules:
  0.0 582.8 jit_solution(1505125445887962174)
XLA Ops:
  9.9 24.3 %all-gather.4.cloned.1.call-done = f32[1024,512]{1,0:T(8,128)} async-done(((f32[1024,128]{1,0:T(8,128)}), f32[1024,512]{1,0:T(8,128)}) %all-gather.4.cloned.1.call-update) | async-done | bytes 2097168 | tf_op jit(solution)/shard_map/all_gather | solution.py:60
  42.0 28.0 %multiply_reduce_fusion.1 = (f32[8,1024]{1,0:T(8,128)S(1)}, f32[8,1024,1024]{1,2,0:T(8,128)S(1)}) fusion(f32[1024,8,16]{0,2,1:T(8,128)S(1)} %fusion.32, f32[1024,8,16]{0,2,1:T(8,128)S(1)} %fusion.30), kind=kOutput, calls=%fused_computation.7 | convolution fusion | flops 1627381760 | bytes 34635776 | tf_op jit(solution)/shard_map/while/body/eval_jaxpr/qhd,khd->hqk/dot_general | solution.py:46
  70.0 5.9 %fusion.4 = f32[8,1024]{1,0:T(8,128)S(1)} fusion(f32[8,1024,1024]{1,2,0:T(8,128)S(1)} %get-tuple-element.80, f32[8,1024]{1,0:T(8,128)S(1)} %get-tuple-element.79), kind=kLoop, calls=%fused_computation.8 | loop fusion | flops 25157632 | bytes 33619968 | tf_op jit(solution)/shard_map/while/body/eval_jaxpr/reduce_sum | solution.py:51
  75.9 5.2 copy-done
  84.4 25.6 %fusion.2 = f32[8,16,1024]{2,1,0:T(8,128)S(1)} fusion(f32[1024,8,16]{0,2,1:T(8,128)} %fusion.34, f32[8,1024,1024]{1,2,0:T(8,128)} %copy-done, f32[8,1024]{1,0:T(8,128)S(1)} %fusion.4, f32[8,1024]{1,0:T(8,128)S(1)} %get-tuple-element.79), kind=kOutput, calls=%fused_computation.4 | convolution fusion | flops 1635778560 | bytes 34668544 | tf_op jit(solution)/shard_map/while/body/eval_jaxpr/hqk,khd->qhd/dot_general | solution.py:52
  110.0 4.1 fusion.299
  114.2 21.4 %all-reduce.5.cloned.1.call-done = f32[1024,512]{1,0:T(8,128)} async-done(((f32[1024,512]{1,0:T(8,128)}), f32[1024,512]{1,0:T(8,128)}) %all-reduce.5.cloned.1.call-update) | async-done | bytes 2097168 | tf_op jit(solution)/shard_map/psum | solution.py:18
  135.7 65.8 %all-reduce.7.cloned.1.call-done = f32[1024,512]{1,0:T(8,128)} async-done(((f32[1024,512]{1,0:T(8,128)}), f32[1024,512]{1,0:T(8,128)}) %all-reduce.7.cloned.1.call-update) | async-done | bytes 2097168 | tf_op jit(solution)/shard_map/psum | solution.py:18
  209.5 9.5 %fusion.14 = f32[1024,512]{1,0:T(8,128)} fusion(f32[1024,512]{1,0:T(8,128)S(1)} %fusion.143, f32[2,512,512]{2,1,0:T(8,128)S(1)} %copy-done.15), kind=kOutput, calls=%fused_computation.20 | convolution fusion | flops 3254779904 | bytes 5242880 | tf_op jit(solution)/shard_map/dot_general | solution.py:56
  220.6 4.3 all-to-all-start
  224.9 25.4 %reduce-scatter.3.cloned.1.call-done = f32[1024,128]{1,0:T(8,128)} async-done(((f32[1024,512]{1,0:T(8,128)}), f32[1024,128]{1,0:T(8,128)}) %reduce-scatter.3.cloned.1.call-update) | async-done | bytes 524304 | tf_op jit(solution)/shard_map/reduce_scatter | solution.py:84
  253.5 4.3 all-to-all-start.1
  259.1 15.6 %all-to-all-done.1 = f32[4,5,64,128]{3,2,1,0:T(8,128)S(1)} async-done(((f32[4,5,64,128]{3,2,1,0:T(8,128)}), f32[4,5,64,128]{3,2,1,0:T(8,128)S(1)}, u32[]{:S(2)}, u32[]{:S(2)}) %all-to-all-start.1) | async-done | bytes 655392 | tf_op jit(solution)/shard_map/all_to_all | solution.py:112
  276.9 21.8 %all-gather.6.cloned.1.call-done = f32[1024,512]{1,0:T(8,128)} async-done(((f32[1024,128]{1,0:T(8,128)}), f32[1024,512]{1,0:T(8,128)}) %all-gather.6.cloned.1.call-update) | async-done | bytes 2097168 | tf_op jit(solution)/shard_map/all_gather | solution.py:60
  306.4 27.9 %multiply_reduce_fusion = (f32[8,1024]{1,0:T(8,128)S(1)}, f32[8,1024,1024]{1,2,0:T(8,128)S(1)}) fusion(f32[1024,8,16]{0,2,1:T(8,128)S(1)} %fusion.26, f32[1024,8,16]{0,2,1:T(8,128)S(1)} %fusion.24), kind=kOutput, calls=%fused_computation.6 | convolution fusion | flops 1627381760 | bytes 34635776 | tf_op jit(solution)/shard_map/while/body/eval_jaxpr/qhd,khd->hqk/dot_general | solution.py:46
  334.4 5.9 %fusion.5 = f32[8,1024]{1,0:T(8,128)S(1)} fusion(f32[8,1024,1024]{1,2,0:T(8,128)S(1)} %get-tuple-element.82, f32[8,1024]{1,0:T(8,128)S(1)} %get-tuple-element.81), kind=kLoop, calls=%fused_computation.9 | loop fusion | flops 25157632 | bytes 33619968 | tf_op jit(solution)/shard_map/while/body/eval_jaxpr/reduce_sum | solution.py:51
  340.3 5.2 copy-done.1
  348.0 25.0 %fusion = f32[8,16,1024]{2,1,0:T(8,128)S(1)} fusion(f32[1024,8,16]{0,2,1:T(8,128)S(1)} %fusion.28, f32[8,1024,1024]{1,2,0:T(8,128)} %copy-done.1, f32[8,1024]{1,0:T(8,128)S(1)} %fusion.5, f32[8,1024]{1,0:T(8,128)S(1)} %get-tuple-element.81), kind=kOutput, calls=%fused_computation.2 | convolution fusion | flops 1635778560 | bytes 34668544 | tf_op jit(solution)/shard_map/while/body/eval_jaxpr/hqk,khd->qhd/dot_general | solution.py:52
  373.0 4.1 fusion.297
  377.2 21.4 %all-reduce.9.cloned.1.call-done = f32[1024,512]{1,0:T(8,128)} async-done(((f32[1024,512]{1,0:T(8,128)}), f32[1024,512]{1,0:T(8,128)}) %all-reduce.9.cloned.1.call-update) | async-done | bytes 2097168 | tf_op jit(solution)/shard_map/psum | solution.py:18
  398.6 65.8 %all-reduce.11.cloned.1.call-done = f32[1024,512]{1,0:T(8,128)} async-done(((f32[1024,512]{1,0:T(8,128)}), f32[1024,512]{1,0:T(8,128)}) %all-reduce.11.cloned.1.call-update) | async-done | bytes 2097168 | tf_op jit(solution)/shard_map/psum | solution.py:18
  472.4 9.5 %fusion.18 = f32[1024,512]{1,0:T(8,128)} fusion(f32[1024,512]{1,0:T(8,128)S(1)} %fusion.89, f32[2,512,512]{2,1,0:T(8,128)S(1)} %copy-done.16), kind=kOutput, calls=%fused_computation.23 | convolution fusion | flops 3254779904 | bytes 5242880 | tf_op jit(solution)/shard_map/dot_general | solution.py:56
  482.0 31.3 %reduce-scatter.5.cloned.1.call-done = f32[1024,128]{1,0:T(8,128)} async-done(((f32[1024,512]{1,0:T(8,128)}), f32[1024,128]{1,0:T(8,128)}) %reduce-scatter.5.cloned.1.call-update) | async-done | bytes 524304 | tf_op jit(solution)/shard_map/reduce_scatter | solution.py:84
  515.6 23.3 %all-gather.8.cloned.1.call-done = f32[1024,512]{1,0:T(8,128)} async-done(((f32[1024,128]{1,0:T(8,128)}), f32[1024,512]{1,0:T(8,128)}) %all-gather.8.cloned.1.call-update) | async-done | bytes 2097168 | tf_op jit(solution)/shard_map/all_gather | solution.py:60
  (142 shorter events, 88.1 us)
Async XLA Ops:
  6.5 27.7 %all-gather.4.cloned.1.call-start = ((), (), s32[]{:S(2)}) async-start(), calls=%async_computation.4 | async-start | bytes 2621440 | tf_op jit(solution)/shard_map/all_gather | solution.py:60
  7.3 128.3 %all-reduce.5.cloned.1.call-start = ((), (), s32[]{:S(2)}) async-start(), calls=%async_computation.5 | async-start | bytes 4194304 | tf_op jit(solution)/shard_map/psum | solution.py:18
  114.1 21.5 %copy-start.11 = (f32[2,512]{1,0:T(2,128)S(1)}, f32[2,512]{1,0:T(2,128)}, u32[]{:S(2)}) copy-start(f32[2,512]{1,0:T(2,128)} %param.19) | copy-start | bytes 12292
  114.2 87.4 %all-reduce.7.cloned.1.call-start = ((), (), s32[]{:S(2)}) async-start(), calls=%async_computation.6 | async-start | bytes 4194304 | tf_op jit(solution)/shard_map/psum | solution.py:18
  135.6 114.7 %reduce-scatter.3.cloned.1.call-start = ((), (), s32[]{:S(2)}) async-start(), calls=%async_computation.7 | async-start | bytes 2621440 | tf_op jit(solution)/shard_map/reduce_scatter | solution.py:84
  220.6 32.8 %all-to-all-start = ((f32[4,1,5]{2,1,0:T(1,128)}), f32[4,1,5]{2,1,0:T(1,128)S(1)}, u32[]{:S(2)}, u32[]{:S(2)}) async-start(f32[4,1,5]{2,1,0:T(1,128)} %bitcast.2), calls=%async_computation | async-start | bytes 4096 | tf_op jit(solution)/shard_map/all_to_all | solution.py:113
  253.5 21.2 %all-to-all-start.1 = ((f32[4,5,64,128]{3,2,1,0:T(8,128)}), f32[4,5,64,128]{3,2,1,0:T(8,128)S(1)}, u32[]{:S(2)}, u32[]{:S(2)}) async-start(f32[4,5,64,128]{3,2,1,0:T(8,128)} %copy.48), calls=%async_computation.2 | async-start | bytes 1310720 | tf_op jit(solution)/shard_map/all_to_all | solution.py:112
  257.8 40.9 %all-gather.6.cloned.1.call-start = ((), (), s32[]{:S(2)}) async-start(), calls=%async_computation.8 | async-start | bytes 2621440 | tf_op jit(solution)/shard_map/all_gather | solution.py:60
  276.4 122.1 %all-reduce.9.cloned.1.call-start = ((), (), s32[]{:S(2)}) async-start(), calls=%async_computation.9 | async-start | bytes 4194304 | tf_op jit(solution)/shard_map/psum | solution.py:18
  377.1 87.3 %all-reduce.11.cloned.1.call-start = ((), (), s32[]{:S(2)}) async-start(), calls=%async_computation.10 | async-start | bytes 4194304 | tf_op jit(solution)/shard_map/psum | solution.py:18
  398.6 114.7 %reduce-scatter.5.cloned.1.call-start = ((), (), s32[]{:S(2)}) async-start(), calls=%async_computation.11 | async-start | bytes 2621440 | tf_op jit(solution)/shard_map/reduce_scatter | solution.py:84
  481.9 33.6 %copy-start.9 = (f32[2,3,3,512]{3,0,2,1:T(2,128)S(1)}, f32[2,3,3,512]{3,0,2,1:T(2,128)}, u32[]{:S(2)}) copy-start(f32[2,3,3,512]{3,0,2,1:T(2,128)} %param.23) | copy-start | bytes 110596
  481.9 57.0 %copy-start.13 = (s32[1024]{0:T(1024)S(1)}, s32[1024]{0:T(1024)}, u32[]{:S(2)}) copy-start(s32[1024]{0:T(1024)} %param.22) | copy-start | bytes 12292
  481.9 57.0 %all-gather.8.cloned.1.call-start = ((), (), s32[]{:S(2)}) async-start(), calls=%async_computation.12 | async-start | bytes 2621440 | tf_op jit(solution)/shard_map/all_gather | solution.py:60
  515.3 38.4 %copy-start.12 = (f32[2,512]{1,0:T(2,128)S(1)}, f32[2,512]{1,0:T(2,128)}, u32[]{:S(2)}) copy-start(f32[2,512]{1,0:T(2,128)} %param.25) | copy-start | bytes 12292
  538.9 18.4 %copy-start.14 = (f32[2,512,1024]{2,1,0:T(8,128)S(1)}, f32[2,512,1024]{2,1,0:T(8,128)}, u32[]{:S(2)}) copy-start(f32[2,512,1024]{2,1,0:T(8,128)} %param.24) | copy-start | bytes 12582916
  541.7 5.2 collective-permute-start
  545.0 5.2 collective-permute-start.1
  550.3 3.5 collective-permute-start.2
  552.5 4.5 collective-permute-start.3
  558.9 5.3 collective-permute-start.4
  562.2 5.2 collective-permute-start.5
  567.5 2.7 collective-permute-start.6
  568.9 4.5 collective-permute-start.7
  (14 other events, 57.8 us)
Sparse Core Ops, SparseCore 0:
  8.9 25.2 all-gather.3
  114.3 21.2 all-reduce.4
  137.9 63.5 all-reduce.6
  219.1 31.1 reduce-scatter.2
  276.5 22.0 all-gather.5
  377.2 21.2 all-reduce.8
  400.8 63.5 all-reduce.10
  482.0 31.1 reduce-scatter.4
  515.5 23.3 all-gather.7
